TPU v7x, 128 devices: a whole 4x4x4 slice. The times are simulated.
128 devices in a mesh: segment: 2 (over core), seq: 32 (over z_lo, y, x), mp: 2 (over z_hi).
Axes of the slice: x: 4, y: 4, z: 4 (z_hi: 2, z_lo: 2; z = z_hi * 2 + z_lo), core: 2. Of those that a mesh axis runs over, the one named last changes fastest.
Arguments:
- inputs: bfloat16 [65536, 512], P('seq', 'mp'), may hold values from -6 to 6
- cotangent: bfloat16 [65536, 512], P('seq', 'mp'), may hold values from -0.375 to 0.375
- gate_gain: float32 [2, 512], P('segment', 'mp'), may hold values from 0.3 to 3
- key_gain: float32 [2, 512], P('segment', 'mp'), may hold values from 0.3 to 3
- first_factor: bfloat16 [2, 256, 256, 256], P('segment', 'seq'), may hold values from -0.375 to 0.375
- second_factor: bfloat16 [2, 256, 256, 256], P('segment', 'seq'), may hold values from -0.375 to 0.375
- up_first: bfloat16 [2, 4, 128, 128], P('segment', 'mp'), may hold values from -0.5 to 0.5
- up_second: bfloat16 [2, 4, 128, 512], P('segment', 'mp'), may hold values from -0.5 to 0.5
- down_first: bfloat16 [2, 4, 512, 128], P('segment', 'mp'), may hold values from -0.25 to 0.25
- down_second_weight: bfloat16 [2, 4, 128, 128], P('segment', 'mp'), may hold values from -0.5 to 0.5
Outputs:
- grad_first: float32 [2, 256, 256, 256], P('segment', 'seq', 'mp')
- grad_second: float32 [2, 256, 256, 256], P('segment', 'seq', 'mp')
All inputs are finite; a program needn't handle non-finite values.
Results may differ from a plain program's by a relative error of at most 0.024.
Values may be sent and summed in bfloat16 or wider, within the bound.
No kernel may reach another device: no remote copies, remote signals or barrier semaphores. Data moves between devices by JAX's collectives and lax.ppermute only.
A program may use at most 128 MiB of HBM per device.

v0:
```python
import jax
import jax.numpy as jnp
from jax import lax
from jax.sharding import PartitionSpec as P


def shifted(value, axis, steps):
    count = lax.axis_size(axis)
    leading, last = (max(0, -steps), min(count, count - steps))
    return lax.ppermute(value, axis, [(source, source + steps) for source in range(leading, last)])


def sigmoid_slope(values):
    logistic = jax.nn.sigmoid(values)
    return logistic * (1.0 + values * (1.0 - logistic))


def sequence_mix(scaled, first_block, second_block):
    mixed_rows = jnp.einsum(
        "aoi,aic->aoc", first_block, scaled, preferred_element_type=jnp.float32
    ).astype(jnp.bfloat16)
    columns = lax.all_to_all(mixed_rows, "seq", split_axis=1, concat_axis=0, tiled=True)
    turned_cols = jnp.einsum(
        "boi,ibc->obc", second_block, columns, preferred_element_type=jnp.float32
    ).astype(jnp.bfloat16)
    return (lax.all_to_all(turned_cols, "seq", split_axis=0, concat_axis=1, tiled=True), columns)


def sequence_back(back_turned, mixed_cols, second_block):
    back_turned_cols = lax.all_to_all(back_turned, "seq", split_axis=1, concat_axis=0, tiled=True)
    second_grad = jnp.einsum(
        "obc,ibc->boi", back_turned_cols, mixed_cols, preferred_element_type=jnp.float32
    )
    back_mixed_cols = jnp.einsum(
        "boi,obc->ibc", second_block, back_turned_cols, preferred_element_type=jnp.float32
    ).astype(jnp.bfloat16)
    back_mixed = lax.all_to_all(back_mixed_cols, "seq", split_axis=0, concat_axis=1, tiled=True)
    return (back_mixed, second_grad)


def forward_pass(rows_in, weights, with_output):
    (
        gate_gain,
        key_gain,
        first_block,
        second_block,
        up_first,
        up_second,
        down_first,
        down_second_weight,
    ) = weights
    tokens = rows_in.shape[0]
    channels = rows_in.shape[1]
    row_blocks = first_block.shape[0]
    block_size = first_block.shape[1]
    local_blocks = up_first.shape[0]
    block_column_width = up_first.shape[1]
    total_blocks = local_blocks * lax.axis_size("mp")
    sub_width = block_column_width // total_blocks
    rows_grid = rows_in.reshape(row_blocks, block_size, channels).astype(jnp.float32)
    scaled = (rows_grid * key_gain).astype(jnp.bfloat16)
    turned, mixed_cols = sequence_mix(scaled, first_block, second_block)
    gate_pre = rows_grid * gate_gain
    hidden_rows = (rows_grid + jax.nn.silu(gate_pre) * turned.astype(jnp.float32)).astype(
        jnp.bfloat16
    )
    hidden_rows = hidden_rows.reshape(tokens, local_blocks, block_column_width)
    up_grid = up_first.reshape(local_blocks, block_column_width, total_blocks, sub_width)
    permuted = jnp.einsum(
        "tki,kijc->tjkc", hidden_rows, up_grid, preferred_element_type=jnp.float32
    ).astype(jnp.bfloat16)
    permuted = permuted.reshape(tokens, total_blocks, local_blocks * sub_width)
    gathered_in = lax.all_to_all(permuted, "mp", split_axis=1, concat_axis=2, tiled=True)
    preact = jnp.einsum("tjq,jqe->tje", gathered_in, up_second, preferred_element_type=jnp.float32)
    kept_state = (rows_grid, scaled, mixed_cols, turned, preact)
    if not with_output:
        return (None, kept_state)
    active = jax.nn.silu(preact).astype(jnp.bfloat16)
    down_grid = down_first.reshape(local_blocks, down_first.shape[1], total_blocks, sub_width)
    folded_rows = jnp.einsum(
        "tje,jemc->tmjc", active, down_grid, preferred_element_type=jnp.float32
    ).astype(jnp.bfloat16)
    folded_rows = folded_rows.reshape(tokens, total_blocks, local_blocks * sub_width)
    gathered_output = lax.all_to_all(folded_rows, "mp", split_axis=1, concat_axis=2, tiled=True)
    output_portion = jnp.einsum(
        "xds,dsl->xdl", gathered_output, down_second_weight, preferred_element_type=jnp.float32
    )
    result = (
        (hidden_rows.astype(jnp.float32) + output_portion)
        .reshape(tokens, channels)
        .astype(jnp.bfloat16)
    )
    return (result, kept_state)


def backward_pass(cot_rows, kept_state, weights):
    (
        gate_gain,
        key_gain,
        first_block,
        second_block,
        up_first,
        up_second,
        down_first,
        down_second_weight,
    ) = weights
    rows_grid, scaled, mixed_cols, turned, preact = kept_state
    tokens = cot_rows.shape[0]
    channels = cot_rows.shape[1]
    row_blocks = first_block.shape[0]
    block_size = first_block.shape[1]
    local_blocks = up_first.shape[0]
    block_column_width = up_first.shape[1]
    total_blocks = local_blocks * lax.axis_size("mp")
    sub_width = block_column_width // total_blocks
    up_grid = up_first.reshape(local_blocks, block_column_width, total_blocks, sub_width)
    down_grid = down_first.reshape(local_blocks, down_first.shape[1], total_blocks, sub_width)
    backward_folded_rows = jnp.einsum(
        "hsd,sad->hsa",
        cot_rows.reshape(tokens, local_blocks, block_column_width),
        down_second_weight,
        preferred_element_type=jnp.float32,
    ).astype(jnp.bfloat16)
    back_grid = lax.all_to_all(
        backward_folded_rows, "mp", split_axis=2, concat_axis=1, tiled=True
    ).reshape(tokens, total_blocks, local_blocks, sub_width)
    back_active = jnp.einsum(
        "tmjc,jemc->tje", back_grid, down_grid, preferred_element_type=jnp.float32
    )
    back_preact = (back_active * sigmoid_slope(preact)).astype(jnp.bfloat16)
    back_perm = jnp.einsum(
        "tje,jqe->tjq", back_preact, up_second, preferred_element_type=jnp.float32
    ).astype(jnp.bfloat16)
    back_perm_grid = lax.all_to_all(
        back_perm, "mp", split_axis=2, concat_axis=1, tiled=True
    ).reshape(tokens, total_blocks, local_blocks, sub_width)
    back_ffn = jnp.einsum(
        "tjkc,kijc->tki", back_perm_grid, up_grid, preferred_element_type=jnp.float32
    )
    back_hidden = cot_rows.astype(jnp.float32).reshape(
        row_blocks, block_size, channels
    ) + back_ffn.reshape(row_blocks, block_size, channels)
    gate_pre = rows_grid * gate_gain
    back_turned = (back_hidden * jax.nn.silu(gate_pre)).astype(jnp.bfloat16)
    back_mixed, second_grad = sequence_back(back_turned, mixed_cols, second_block)
    first_grad = jnp.einsum("aoc,aic->aoi", back_mixed, scaled, preferred_element_type=jnp.float32)
    back_scaled = jnp.einsum(
        "aoi,aoc->aic", first_block, back_mixed, preferred_element_type=jnp.float32
    )
    back_inputs = (
        back_hidden
        + back_hidden * turned.astype(jnp.float32) * sigmoid_slope(gate_pre) * gate_gain
        + back_scaled * key_gain
    )
    back_inputs = back_inputs.reshape(tokens, channels).astype(jnp.bfloat16)
    return (back_inputs, first_grad, second_grad)


def reduce_channels(first_grad, second_grad):
    totals_first, totals_second = (
        lax.psum(first_grad.astype(jnp.bfloat16), "mp").astype(jnp.float32),
        lax.psum(second_grad.astype(jnp.bfloat16), "mp").astype(jnp.float32),
    )
    half_rows = first_grad.shape[2] // lax.axis_size("mp")
    offset = lax.axis_index("mp") * half_rows
    share_first = lax.dynamic_slice_in_dim(totals_first, offset, half_rows, 2)
    share_second = lax.dynamic_slice_in_dim(totals_second, offset, half_rows, 2)
    return (share_first, share_second)


def on_device(
    inputs,
    cotangent,
    gate_gain,
    key_gain,
    first_factor,
    second_factor,
    up_first,
    up_second,
    down_first,
    down_second_weight,
):
    weights = (
        gate_gain[0],
        key_gain[0],
        first_factor[0],
        second_factor[0],
        up_first[0],
        up_second[0],
        down_first[0],
        down_second_weight[0],
    )
    early_out, early_state = forward_pass(inputs, weights, True)
    received = shifted(early_out, "segment", 1)
    unused_late, later_state = forward_pass(received, weights, False)
    is_first = lax.axis_index("segment") == 0

    def choose_segment(former, latter):
        return jnp.where(is_first, former, latter)

    kept_state = jax.tree.map(choose_segment, early_state, later_state)
    back_upper, first_upper, second_upper = backward_pass(cotangent, kept_state, weights)
    sent_back = shifted(back_upper, "segment", -1)
    back_lower, first_lower, second_lower = backward_pass(sent_back, kept_state, weights)
    first_grad = jnp.where(is_first, first_lower, first_upper)
    second_grad = jnp.where(is_first, second_lower, second_upper)
    return reduce_channels(first_grad[None], second_grad[None])


def solution(mesh):
    placed = (
        P("seq", "mp"),
        P("seq", "mp"),
        P("segment", "mp"),
        P("segment", "mp"),
        P("segment", "seq", None, None),
        P("segment", "seq", None, None),
        P("segment", "mp", None, None),
        P("segment", "mp", None, None),
        P("segment", "mp", None, None),
        P("segment", "mp", None, None),
    )
    return jax.shard_map(
        on_device,
        mesh=mesh,
        in_specs=placed,
        out_specs=(P("segment", "seq", "mp", None), P("segment", "seq", "mp", None)),
        check_vma=False,
    )
```

profile of v0, /device:TPU:1, one launch (start us, length us, event | category | flops | bytes accessed | tf_op | source)
XLA Modules:
  0.0 530.9 jit_solution(14439777909356738681)
XLA Ops:
  11.6 2.6 copy.178
  14.2 24.8 %all_to_all.240 = bf16[8,256,256]{2,0,1:T(8,128)(2,1)S(1)} all-to-all(bf16[8,256,256]{2,0,1:T(8,128)(2,1)} %copy.178), channel_id=1, replica_groups=mesh['segment'=2,'seq'=32,'mp'=2] {'seq'}, dimensions={1} | all-to-all | bytes 2097152 | tf_op jit(solution)/shard_map/all_to_all | solution.py:22
  41.8 2.6 copy.182
  44.5 4.7 all-to-all-start.2
  49.1 2.6 copy.176
  51.8 11.6 %all-to-all-done.2 = bf16[256,8,256]{2,1,0:T(8,128)(2,1)} async-done(((bf16[256,8,256]{2,1,0:T(8,128)(2,1)}), bf16[256,8,256]{2,1,0:T(8,128)(2,1)}, u32[]{:S(2)}, u32[]{:S(2)}) %all-to-all-start.2) | async-done | bytes 1048608 | tf_op jit(solution)/shard_map/all_to_all | solution.py:26
  66.4 3.3 reshape.116
  69.6 4.2 copy.184
  73.8 3.0 add_convert_fusion.1
  77.6 15.9 %all_to_all.241 = bf16[2048,4,64]{0,2,1:T(8,128)(2,1)S(1)} all-to-all(bf16[2048,4,64]{0,2,1:T(8,128)(2,1)S(1)} %bitcast.283), channel_id=1, replica_groups=mesh['segment'=2,'seq'=32,'mp'=2] {'mp'}, dimensions={1} | all-to-all | bytes 2097152 | tf_op jit(solution)/shard_map/all_to_all | solution.py:73
  94.9 2.8 fusion.6
  98.4 13.1 %all_to_all.242 = bf16[2048,4,64]{0,2,1:T(8,128)(2,1)S(1)} all-to-all(bf16[2048,4,64]{0,2,1:T(8,128)(2,1)S(1)} %bitcast.285), channel_id=1, replica_groups=mesh['segment'=2,'seq'=32,'mp'=2] {'mp'}, dimensions={1} | all-to-all | bytes 2097152 | tf_op jit(solution)/shard_map/all_to_all | solution.py:84
  113.4 7.8 %collective-permute-done = bf16[2048,256]{0,1:T(8,128)(2,1)} collective-permute-done((bf16[2048,256]{0,1:T(8,128)(2,1)S(1)}, bf16[2048,256]{0,1:T(8,128)(2,1)}, u32[]{:S(2)}, u32[]{:S(2)}) %collective-permute-start) | collective-permute-done | bytes 1048608 | tf_op jit(solution)/shard_map/ppermute | solution.py:10
  121.2 2.6 copy.194
  123.8 1.9 multiply_convert_fusion.2
  128.2 2.6 copy.196
  130.8 22.3 %all_to_all.243 = bf16[8,256,256]{2,0,1:T(8,128)(2,1)S(1)} all-to-all(bf16[8,256,256]{2,0,1:T(8,128)(2,1)} %copy.196), channel_id=1, replica_groups=mesh['segment'=2,'seq'=32,'mp'=2] {'seq'}, dimensions={1} | all-to-all | bytes 2097152 | tf_op jit(solution)/shard_map/all_to_all | solution.py:22
  155.9 2.6 copy.200
  158.5 4.7 all-to-all-start.6
  164.9 2.1 copy.171
  167.0 2.8 convert_element_type.273
  169.8 8.2 %all-to-all-done.6 = bf16[256,8,256]{2,1,0:T(8,128)(2,1)} async-done(((bf16[256,8,256]{2,1,0:T(8,128)(2,1)}), bf16[256,8,256]{2,1,0:T(8,128)(2,1)}, u32[]{:S(2)}, u32[]{:S(2)}) %all-to-all-start.6) | async-done | bytes 1048608 | tf_op jit(solution)/shard_map/all_to_all | solution.py:26
  177.9 4.4 all-to-all-start
  185.3 3.3 reshape.119
  188.6 4.2 copy.202
  192.8 3.2 fusion.43
  197.2 4.4 all-to-all-start.7
  201.7 1.8 copy.174
  206.1 7.5 %all-to-all-done.7 = bf16[2048,4,64]{0,2,1:T(8,128)(2,1)} async-done(((bf16[2048,4,64]{0,2,1:T(8,128)(2,1)}), bf16[2048,4,64]{0,2,1:T(8,128)(2,1)}, u32[]{:S(2)}, u32[]{:S(2)}) %all-to-all-start.7) | async-done | bytes 1048608 | tf_op jit(solution)/shard_map/all_to_all | solution.py:73
  214.9 7.5 %add_multiply_fusion = f32[2048,2,512]{2,0,1:T(8,128)} fusion(f32[2,2048,512]{2,1,0:T(8,128)} %copy-done.5, bf16[2048,2,128]{0,2,1:T(8,128)(2,1)S(1)} %bitcast.301, pred[]{:T(512)S(6)} %eq.3, bf16[1,2,128,512]{3,2,1,0:T(8,128)(2,1)S(1)} %copy-done.18), kind=kOutput, calls=%fused_computation.10 | convolution fusion | flops 553648128 | bytes 18087936 | tf_op jit(solution)/shard_map/tjq,jqe->tje/dot_general | solution.py:74
  222.4 7.1 %fusion.12 = bf16[2048,2,128]{2,0,1:T(8,128)(2,1)} fusion(f32[2048,2,512]{2,0,1:T(8,128)} %add_multiply_fusion, bf16[2048,4,2,32]{0,3,2,1:T(8,128)(2,1)} %bitcast.298, bf16[1,2,128,512]{3,2,1,0:T(8,128)(2,1)S(1)} %copy-done.18, bf16[2,512,4,32]{1,3,2,0:T(8,128)(2,1)} %bitcast.305), kind=kOutput, calls=%fused_computation.24 | convolution fusion | flops 1078460416 | bytes 11010048 | tf_op jit(solution)/shard_map/tje,jqe->tjq/dot_general | solution.py:131
  229.5 3.7 copy.207
  233.2 4.6 all-to-all-start.8
  238.8 10.1 %all-to-all-done.8 = bf16[2048,2,128]{0,1,2:T(2,128)(2,1)} async-done(((bf16[2048,2,128]{0,1,2:T(2,128)(2,1)}), bf16[2048,2,128]{0,1,2:T(2,128)(2,1)}, u32[]{:S(2)}, u32[]{:S(2)}) %all-to-all-start.8) | async-done | bytes 1048608 | tf_op jit(solution)/shard_map/all_to_all | solution.py:134
  251.0 8.6 %copy.255 = f32[2048,2,128]{2,1,0:T(2,128)} copy(f32[2048,2,128]{2,0,1:T(8,128)S(1)} %convolution_bitcast_fusion.1) | data formatting | bytes 4194304 | tf_op jit(solution)/shard_map/reshape | solution.py:142
  259.6 3.9 reshape.136
  263.5 3.3 multiply_convert_fusion.1
  267.4 20.8 %all_to_all.244 = bf16[8,256,256]{2,0,1:T(8,128)(2,1)S(1)} all-to-all(bf16[8,256,256]{2,0,1:T(8,128)(2,1)S(1)} %copy.214), channel_id=1, replica_groups=mesh['segment'=2,'seq'=32,'mp'=2] {'seq'}, dimensions={1} | all-to-all | bytes 2097152 | tf_op jit(solution)/shard_map/all_to_all | solution.py:30
  291.0 2.6 copy.218
  293.7 5.0 all-to-all-start.10
  298.6 2.3 broadcast_select_fusion.1
  301.0 10.3 %all-to-all-done.10 = bf16[256,8,256]{2,1,0:T(8,128)(2,1)} async-done(((bf16[256,8,256]{2,1,0:T(8,128)(2,1)}), bf16[256,8,256]{2,1,0:T(8,128)(2,1)}, u32[]{:S(2)}, u32[]{:S(2)}) %all-to-all-start.10) | async-done | bytes 1048608 | tf_op jit(solution)/shard_map/all_to_all | solution.py:37
  311.3 6.2 %fusion.14 = bf16[8,256,256]{2,1,0:T(8,128)(2,1)} fusion(f32[8,256,256]{2,1,0:T(8,128)} %reshape.136, bf16[8,256,256]{2,1,0:T(8,128)(2,1)} %bitcast.271, bf16[1,8,256,256]{3,2,1,0:T(8,128)(2,1)} %param.14, f32[256]{0:T(256)S(1)} %bitcast.314, f32[256]{0:T(256)S(1)} %bitcast.310, bf16[8,32,8,256]{3,2,0,1:T(8,128)(2,1)} %bitcast.76, ...), kind=kOutput, calls=%fused_computation.31 | convolution fusion | flops 278396928 | bytes 11536385 | tf_op jit(solution)/shard_map/aoi,aoc->aic/dot_general | solution.py:147
  317.5 2.3 copy.221
  319.7 6.8 %collective-permute-start.1 = (bf16[2048,256]{0,1:T(8,128)(2,1)}, bf16[2048,256]{0,1:T(8,128)(2,1)S(1)}, u32[]{:S(2)}, u32[]{:S(2)}) collective-permute-start(bf16[2048,256]{0,1:T(8,128)(2,1)} %copy.221), channel_id=1, source_target_pairs={{64,0},{65,1},{66,2},{67,3},{68,4},{69,5},{70,6},{71,7},{72,8},{73... | collective-permute-start | bytes 3145736 | tf_op jit(solution)/shard_map/ppermute | solution.py:10
  326.5 2.0 collective-permute-done.1
  331.0 3.7 copy.224
  334.7 18.4 %all_to_all.245 = bf16[2048,2,128]{0,1,2:T(2,128)(2,1)S(1)} all-to-all(bf16[2048,2,128]{0,1,2:T(2,128)(2,1)} %copy.224), channel_id=1, replica_groups=mesh['segment'=2,'seq'=32,'mp'=2] {'mp'}, dimensions={2} | all-to-all | bytes 2097152 | tf_op jit(solution)/shard_map/all_to_all | solution.py:124
  354.5 7.2 %fusion.13 = bf16[2048,2,128]{2,0,1:T(8,128)(2,1)} fusion(f32[2048,2,512]{2,0,1:T(8,128)} %add_multiply_fusion, bf16[2048,4,2,32]{0,3,2,1:T(8,128)(2,1)} %bitcast.300, bf16[1,2,128,512]{3,2,1,0:T(8,128)(2,1)S(1)} %copy-done.18, bf16[2,512,4,32]{1,3,2,0:T(8,128)(2,1)} %bitcast.306), kind=kOutput, calls=%fused_computation.25 | convolution fusion | flops 1078460416 | bytes 11010048 | tf_op jit(solution)/shard_map/tje,jqe->tjq/dot_general | solution.py:131
  361.6 3.7 copy.228
  365.3 4.4 all-to-all-start.12
  369.7 2.6 copy.222
  372.3 11.4 %all-to-all-done.12 = bf16[2048,2,128]{0,1,2:T(2,128)(2,1)} async-done(((bf16[2048,2,128]{0,1,2:T(2,128)(2,1)}), bf16[2048,2,128]{0,1,2:T(2,128)(2,1)}, u32[]{:S(2)}, u32[]{:S(2)}) %all-to-all-start.12) | async-done | bytes 1048608 | tf_op jit(solution)/shard_map/all_to_all | solution.py:134
  386.0 8.6 %copy.232 = f32[2048,2,128]{2,1,0:T(2,128)} copy(f32[2048,2,128]{2,0,1:T(8,128)S(1)} %convolution_bitcast_fusion) | data formatting | bytes 4194304 | tf_op jit(solution)/shard_map/tjkc,kijc->tki/transpose | solution.py:137
  394.6 3.9 reshape.111
  398.4 3.5 multiply_convert_fusion
  402.6 18.7 %all_to_all.246 = bf16[8,256,256]{2,0,1:T(8,128)(2,1)S(1)} all-to-all(bf16[8,256,256]{2,0,1:T(8,128)(2,1)S(1)} %copy.233), channel_id=1, replica_groups=mesh['segment'=2,'seq'=32,'mp'=2] {'seq'}, dimensions={1} | all-to-all | bytes 2097152 | tf_op jit(solution)/shard_map/all_to_all | solution.py:30
  424.1 2.8 copy.237
  426.9 4.9 all-to-all-start.14
  435.9 9.5 %all-to-all-done.14 = bf16[256,8,256]{2,1,0:T(8,128)(2,1)} async-done(((bf16[256,8,256]{2,1,0:T(8,128)(2,1)}), bf16[256,8,256]{2,1,0:T(8,128)(2,1)}, u32[]{:S(2)}, u32[]{:S(2)}) %all-to-all-start.14) | async-done | bytes 1048608 | tf_op jit(solution)/shard_map/all_to_all | solution.py:37
  445.4 1.8 fusion.29
  447.1 2.8 fusion.25
  449.9 71.2 %all-reduce.3.cloned.1.call-done = (bf16[1,8,256,256]{3,2,1,0:T(8,128)(2,1)}, bf16[1,8,256,256]{3,2,1,0:T(8,128)(2,1)}) async-done(((bf16[1,8,256,256]{3,2,1,0:T(8,128)(2,1)}, bf16[1,8,256,256]{3,2,1,0:T(8,128)(2,1)}), (bf16[1,8,256,256]{3,2,1,0:T(8,128)(2,1)}, bf16[1,8,256,256]{3,2,1,0:T(8,128)(2,1)})) %all-reduce.3.cloned.1.call-update) | async-done | bytes 2097168 | tf_op jit(solution)/shard_map/psum | solution.py:161
  521.1 2.7 dynamic-slice_convert_fusion
  (96 shorter events, 49.9 us)
Async XLA Ops:
  7.2 33.2 %copy-start = (bf16[1,8,256,256]{3,2,1,0:T(8,128)(2,1)S(1)}, bf16[1,8,256,256]{3,2,1,0:T(8,128)(2,1)}, u32[]{:S(2)}) copy-start(bf16[1,8,256,256]{3,2,1,0:T(8,128)(2,1)} %param.15) | copy-start | bytes 3145732
  7.2 1.5 copy-start.22
  8.7 1.5 copy-start.6
  8.9 1.0 copy-start.8
  39.4 1.0 copy-start.1
  44.5 18.9 %all-to-all-start.2 = ((bf16[256,8,256]{2,1,0:T(8,128)(2,1)}), bf16[256,8,256]{2,1,0:T(8,128)(2,1)}, u32[]{:S(2)}, u32[]{:S(2)}) async-start(bf16[256,8,256]{2,1,0:T(8,128)(2,1)} %copy.182), calls=%async_computation.2 | async-start | bytes 2097152 | tf_op jit(solution)/shard_map/all_to_all | solution.py:26
  69.6 4.2 copy-start.21
  73.8 3.0 copy-start.19
  77.6 16.0 %copy-start.18 = (bf16[1,2,128,512]{3,2,1,0:T(8,128)(2,1)S(1)}, bf16[1,2,128,512]{3,2,1,0:T(8,128)(2,1)}, u32[]{:S(2)}) copy-start(bf16[1,2,128,512]{3,2,1,0:T(8,128)(2,1)} %param.17) | copy-start | bytes 786436
  93.5 1.3 copy-start.20
  94.9 3.3 copy-start.5
  98.4 13.2 %copy-start.17 = (bf16[1,2,128,128]{3,2,1,0:T(8,128)(2,1)S(1)}, bf16[1,2,128,128]{3,2,1,0:T(8,128)(2,1)}, u32[]{:S(2)}) copy-start(bf16[1,2,128,128]{3,2,1,0:T(8,128)(2,1)} %param.19) | copy-start | bytes 196612
  112.1 9.1 %collective-permute-start = (bf16[2048,256]{0,1:T(8,128)(2,1)S(1)}, bf16[2048,256]{0,1:T(8,128)(2,1)}, u32[]{:S(2)}, u32[]{:S(2)}) collective-permute-start(bf16[2048,256]{0,1:T(8,128)(2,1)S(1)} %bitcast.297), channel_id=1, source_target_pairs={{0,64},{1,65},{2,66},{3,67},{4,68},{5,69},{6,70},{7,71},{8,72},{9,... | collective-permute-start | bytes 3145736 | tf_op jit(solution)/shard_map/ppermute | solution.py:10
  123.8 2.9 copy-start.7
  125.7 1.0 copy-start.10
  153.4 1.0 copy-start.3
  158.5 19.4 %all-to-all-start.6 = ((bf16[256,8,256]{2,1,0:T(8,128)(2,1)}), bf16[256,8,256]{2,1,0:T(8,128)(2,1)}, u32[]{:S(2)}, u32[]{:S(2)}) async-start(bf16[256,8,256]{2,1,0:T(8,128)(2,1)} %copy.200), calls=%async_computation.6 | async-start | bytes 2097152 | tf_op jit(solution)/shard_map/all_to_all | solution.py:26
  177.9 19.3 %all-to-all-start = ((bf16[2048,2,128]{0,1,2:T(2,128)(2,1)}), bf16[2048,2,128]{0,1,2:T(2,128)(2,1)}, u32[]{:S(2)}, u32[]{:S(2)}) async-start(bf16[2048,2,128]{0,1,2:T(2,128)(2,1)} %copy.171), calls=%async_computation | async-start | bytes 2097152 | tf_op jit(solution)/shard_map/all_to_all | solution.py:124
  197.2 16.3 %all-to-all-start.7 = ((bf16[2048,4,64]{0,2,1:T(8,128)(2,1)}), bf16[2048,4,64]{0,2,1:T(8,128)(2,1)}, u32[]{:S(2)}, u32[]{:S(2)}) async-start(bf16[2048,4,64]{0,2,1:T(8,128)(2,1)} %bitcast.281), calls=%async_computation.7 | async-start | bytes 2097152 | tf_op jit(solution)/shard_map/all_to_all | solution.py:73
  233.2 15.7 %all-to-all-start.8 = ((bf16[2048,2,128]{0,1,2:T(2,128)(2,1)}), bf16[2048,2,128]{0,1,2:T(2,128)(2,1)}, u32[]{:S(2)}, u32[]{:S(2)}) async-start(bf16[2048,2,128]{0,1,2:T(2,128)(2,1)} %copy.207), calls=%async_computation.8 | async-start | bytes 2097152 | tf_op jit(solution)/shard_map/all_to_all | solution.py:134
  288.5 1.1 copy-start.12
  293.7 17.6 %all-to-all-start.10 = ((bf16[256,8,256]{2,1,0:T(8,128)(2,1)}), bf16[256,8,256]{2,1,0:T(8,128)(2,1)}, u32[]{:S(2)}, u32[]{:S(2)}) async-start(bf16[256,8,256]{2,1,0:T(8,128)(2,1)} %copy.218), calls=%async_computation.10 | async-start | bytes 2097152 | tf_op jit(solution)/shard_map/all_to_all | solution.py:37
  319.7 8.8 %collective-permute-start.1 = (bf16[2048,256]{0,1:T(8,128)(2,1)}, bf16[2048,256]{0,1:T(8,128)(2,1)S(1)}, u32[]{:S(2)}, u32[]{:S(2)}) collective-permute-start(bf16[2048,256]{0,1:T(8,128)(2,1)} %copy.221), channel_id=1, source_target_pairs={{64,0},{65,1},{66,2},{67,3},{68,4},{69,5},{70,6},{71,7},{72,8},{73... | collective-permute-start | bytes 3145736 | tf_op jit(solution)/shard_map/ppermute | solution.py:10
  328.5 1.0 copy-start.14
  365.3 18.5 %all-to-all-start.12 = ((bf16[2048,2,128]{0,1,2:T(2,128)(2,1)}), bf16[2048,2,128]{0,1,2:T(2,128)(2,1)}, u32[]{:S(2)}, u32[]{:S(2)}) async-start(bf16[2048,2,128]{0,1,2:T(2,128)(2,1)} %copy.228), calls=%async_computation.12 | async-start | bytes 2097152 | tf_op jit(solution)/shard_map/all_to_all | solution.py:134
  421.6 1.0 copy-start.15
  424.1 7.7 %copy-start.2 = (bf16[32,8,8,256]{3,2,1,0:T(8,128)(2,1)S(1)}, bf16[32,8,8,256]{3,2,1,0:T(8,128)(2,1)}, u32[]{:S(2)}) copy-start(bf16[32,8,8,256]{3,2,1,0:T(8,128)(2,1)} %copy-done.1) | copy-start | bytes 3145732
  424.1 7.7 %copy-start.4 = (bf16[32,8,8,256]{3,2,1,0:T(8,128)(2,1)S(1)}, bf16[32,8,8,256]{3,2,1,0:T(8,128)(2,1)}, u32[]{:S(2)}) copy-start(bf16[32,8,8,256]{3,2,1,0:T(8,128)(2,1)} %copy-done.3) | copy-start | bytes 3145732
  426.9 18.5 %all-to-all-start.14 = ((bf16[256,8,256]{2,1,0:T(8,128)(2,1)}), bf16[256,8,256]{2,1,0:T(8,128)(2,1)}, u32[]{:S(2)}, u32[]{:S(2)}) async-start(bf16[256,8,256]{2,1,0:T(8,128)(2,1)} %copy.237), calls=%async_computation.14 | async-start | bytes 2097152 | tf_op jit(solution)/shard_map/all_to_all | solution.py:37
  431.8 89.4 %all-reduce.3.cloned.1.call-start = ((), (), s32[]{:S(2)}) async-start(), calls=%async_computation.15 | async-start | bytes 4194304 | tf_op jit(solution)/shard_map/psum | solution.py:161
  431.8 1.2 copy-start.16
  433.1 1.2 copy-start.13
  434.3 11.1 %copy-start.9 = (bf16[8,256,256]{2,1,0:T(8,128)(2,1)S(1)}, bf16[8,256,256]{2,1,0:T(8,128)(2,1)}, u32[]{:S(2)}) copy-start(bf16[8,256,256]{2,1,0:T(8,128)(2,1)} %copy-done.8) | copy-start | bytes 3145732
  434.3 11.1 %copy-start.11 = (bf16[8,256,256]{2,1,0:T(8,128)(2,1)S(1)}, bf16[8,256,256]{2,1,0:T(8,128)(2,1)}, u32[]{:S(2)}) copy-start(bf16[8,256,256]{2,1,0:T(8,128)(2,1)} %copy-done.10) | copy-start | bytes 3145732
Sparse Core Ops, SparseCore 0:
  450.0 71.0 all-reduce.2
where the time goes:
time: 542 us; the launch traced here: 531 us
  waiting for transfers between devices  150 us (28%)
  blocking collectives  134 us (25%)
  local copies, waits for them, and re-layouts  107 us (20%)
  matrix products  55.9 us (10%)
  starting transfers between devices  45.2 us (8%)
  other arithmetic  24.8 us (5%)
  between operations  14.8 us (3%)
    psum x1, waiting for transfers between devices, reduce_channels(): lax.psum(first_grad.astype(jnp.bfloat16), 'mp').astype(jnp.float32)  71.2 us
    all_to_all x2, blocking collectives, sequence_mix(): lax.all_to_all(mixed_rows, 'seq', split_axis=1, concat_axis=0, tiled=True)  47.1 us
    all_to_all x2, blocking collectives, sequence_back(): lax.all_to_all(back_turned, 'seq', split_axis=1, concat_axis=0, tiled=True)  39.5 us
    all_to_all x2, waiting for transfers between devices, backward_pass(): lax.all_to_all(back_perm, 'mp', split_axis=2, concat_axis=1, tiled=True)  21.5 us
    all_to_all x2, waiting for transfers between devices, sequence_back(): lax.all_to_all(back_mixed_cols, 'seq', split_axis=0, concat_axis=1, tiled...  19.8 us
    all_to_all x2, waiting for transfers between devices, sequence_mix(): lax.all_to_all(turned_cols, 'seq', split_axis=0, concat_axis=1, tiled=True)  19.8 us
    all_to_all x1, blocking collectives, backward_pass(): lax.all_to_all(backward_folded_rows, 'mp', split_axis=2, concat_axis=1, t...  18.4 us
    convert_element_type x6, local copies, waits for them, and re-layouts, forward_pass(): turned.astype(jnp.float32)  17.9 us
  transfers between devices with their start and end apart: 11, of which 10 were waited for; matrix products, arithmetic and copies ran while one was open for 7% of the time, Pallas kernels for 0%

commit v1 on v0

--- a/solution.py
+++ b/solution.py
@@ -23,7 +23,15 @@
     turned_cols = jnp.einsum(
         "boi,ibc->obc", second_block, columns, preferred_element_type=jnp.float32
     ).astype(jnp.bfloat16)
-    return (lax.all_to_all(turned_cols, "seq", split_axis=0, concat_axis=1, tiled=True), columns)
+    return (
+        jnp.concatenate(
+            lax.all_to_all(
+                jnp.stack(jnp.split(turned_cols, lax.axis_size("seq"), axis=0)), "seq", 0, 0
+            ),
+            axis=1,
+        ),
+        columns,
+    )
 
 
 def sequence_back(back_turned, mixed_cols, second_block):

time: 542 us -> 573 us (1.057)
  local copies, waits for them, and re-layouts: 107 us -> 138 us
  blocking collectives: 134 us -> 152 us
  waiting for transfers between devices: 150 us -> 139 us
    unnamed x48 -> x116, local copies, waits for them, and re-layouts: 12.2 us -> 46.9 us
    all_to_all x0 -> x1, blocking collectives: none -> 17.9 us  [sequence_back(): lax.all_to_all(back_mixed_cols, 'seq', split_axis=0, concat_axis=1, tiled...]
    all_to_all x2 -> x1, waiting for transfers between devices: 19.8 us -> 9.94 us  [sequence_back(): lax.all_to_all(back_mixed_cols, 'seq', split_axis=0, concat_axis=1, tiled...]
  transfers between devices with their start and end apart: 11 -> 10, of which waited for: 10 -> 9; matrix products, arithmetic and copies ran while one was open for 7% -> 7% of each run, Pallas kernels for 0% -> 0%
where the time goes in v1:
time: 573 us; the launch traced here: 563 us
  blocking collectives  152 us (27%)
  waiting for transfers between devices  139 us (24%)
  local copies, waits for them, and re-layouts  138 us (24%)
  matrix products  54.4 us (9%)
  starting transfers between devices  40.7 us (7%)
  other arithmetic  24.2 us (4%)
  between operations  14.8 us (3%)
    psum x1, waiting for transfers between devices, reduce_channels(): lax.psum(first_grad.astype(jnp.bfloat16), 'mp').astype(jnp.float32)  70.9 us
    all_to_all x2, blocking collectives, sequence_mix(): lax.all_to_all(mixed_rows, 'seq', split_axis=1, concat_axis=0, tiled=True)  47.1 us
    unnamed x116, local copies, waits for them, and re-layouts  46.9 us
    all_to_all x2, blocking collectives, sequence_back(): lax.all_to_all(back_turned, 'seq', split_axis=1, concat_axis=0, tiled=True)  39.5 us
    all_to_all x2, waiting for transfers between devices, backward_pass(): lax.all_to_all(back_perm, 'mp', split_axis=2, concat_axis=1, tiled=True)  21.2 us
    all_to_all x2, waiting for transfers between devices, sequence_mix(): lax.all_to_all(jnp.stack(jnp.split(turned_cols, lax.axis_size('seq'), axi...  19.8 us
    convert_element_type x6, local copies, waits for them, and re-layouts, forward_pass(): turned.astype(jnp.float32)  18.9 us
    all_to_all x1, blocking collectives, backward_pass(): lax.all_to_all(backward_folded_rows, 'mp', split_axis=2, concat_axis=1, t...  18.4 us
  transfers between devices with their start and end apart: 10, of which 9 were waited for; matrix products, arithmetic and copies ran while one was open for 7% of the time, Pallas kernels for 0%

profile of v1, /device:TPU:1, one launch (start us, length us, event | category | flops | bytes accessed | tf_op | source)
XLA Modules:
  0.0 562.5 jit_solution(5355308728508289790)
XLA Ops:
  11.6 2.6 copy.159
  14.2 24.8 %all_to_all.232 = bf16[8,256,256]{2,0,1:T(8,128)(2,1)S(1)} all-to-all(bf16[8,256,256]{2,0,1:T(8,128)(2,1)} %copy.159), channel_id=1, replica_groups=mesh['segment'=2,'seq'=32,'mp'=2] {'seq'}, dimensions={1} | all-to-all | bytes 2097152 | tf_op jit(solution)/shard_map/all_to_all | solution.py:22
  59.3 4.7 all-to-all-start.2
  64.0 2.6 copy.157
  66.6 11.6 %all-to-all-done.2 = bf16[32,8,8,256]{3,1,2,0:T(8,128)(2,1)} async-done(((bf16[32,8,8,256]{3,1,2,0:T(8,128)(2,1)}), bf16[32,8,8,256]{3,1,2,0:T(8,128)(2,1)}, u32[]{:S(2)}, u32[]{:S(2)}) %all-to-all-start.2) | async-done | bytes 1048608 | tf_op jit(solution)/shard_map/all_to_all | solution.py:28
  79.7 2.0 copy.162
  81.7 3.3 reshape.112
  84.9 4.2 copy.163
  89.2 3.0 add_convert_fusion.1
  92.9 15.9 %all_to_all.233 = bf16[2048,4,64]{0,2,1:T(8,128)(2,1)S(1)} all-to-all(bf16[2048,4,64]{0,2,1:T(8,128)(2,1)S(1)} %bitcast.534), channel_id=1, replica_groups=mesh['segment'=2,'seq'=32,'mp'=2] {'mp'}, dimensions={1} | all-to-all | bytes 2097152 | tf_op jit(solution)/shard_map/all_to_all | solution.py:81
  110.3 2.8 fusion.6
  113.8 13.1 %all_to_all.234 = bf16[2048,4,64]{0,2,1:T(8,128)(2,1)S(1)} all-to-all(bf16[2048,4,64]{0,2,1:T(8,128)(2,1)S(1)} %bitcast.536), channel_id=1, replica_groups=mesh['segment'=2,'seq'=32,'mp'=2] {'mp'}, dimensions={1} | all-to-all | bytes 2097152 | tf_op jit(solution)/shard_map/all_to_all | solution.py:92
  128.8 7.8 %collective-permute-done = bf16[2048,256]{0,1:T(8,128)(2,1)} collective-permute-done((bf16[2048,256]{0,1:T(8,128)(2,1)S(1)}, bf16[2048,256]{0,1:T(8,128)(2,1)}, u32[]{:S(2)}, u32[]{:S(2)}) %collective-permute-start) | collective-permute-done | bytes 1048608 | tf_op jit(solution)/shard_map/ppermute | solution.py:10
  136.6 2.6 copy.173
  139.2 1.9 multiply_convert_fusion.2
  143.5 2.6 copy.175
  146.2 22.3 %all_to_all.235 = bf16[8,256,256]{2,0,1:T(8,128)(2,1)S(1)} all-to-all(bf16[8,256,256]{2,0,1:T(8,128)(2,1)} %copy.175), channel_id=1, replica_groups=mesh['segment'=2,'seq'=32,'mp'=2] {'seq'}, dimensions={1} | all-to-all | bytes 2097152 | tf_op jit(solution)/shard_map/all_to_all | solution.py:22
  188.7 4.7 all-to-all-start.6
  193.4 1.7 fusion.10
  195.1 2.0 copy.152
  197.1 2.8 convert_element_type.261
  199.9 8.2 %all-to-all-done.6 = bf16[32,8,8,256]{3,1,2,0:T(8,128)(2,1)} async-done(((bf16[32,8,8,256]{3,1,2,0:T(8,128)(2,1)}), bf16[32,8,8,256]{3,1,2,0:T(8,128)(2,1)}, u32[]{:S(2)}, u32[]{:S(2)}) %all-to-all-start.6) | async-done | bytes 1048608 | tf_op jit(solution)/shard_map/all_to_all | solution.py:28
  208.1 4.4 all-to-all-start
  212.6 3.5 convert_bitcast_fusion
  216.1 1.9 copy.178
  218.0 3.3 reshape.115
  221.3 4.1 copy.179
  225.4 3.2 fusion.43
  229.8 4.4 all-to-all-start.7
  234.3 1.8 copy.155
  238.7 7.2 %all-to-all-done.7 = bf16[2048,4,64]{0,2,1:T(8,128)(2,1)} async-done(((bf16[2048,4,64]{0,2,1:T(8,128)(2,1)}), bf16[2048,4,64]{0,2,1:T(8,128)(2,1)}, u32[]{:S(2)}, u32[]{:S(2)}) %all-to-all-start.7) | async-done | bytes 1048608 | tf_op jit(solution)/shard_map/all_to_all | solution.py:81
  247.2 7.5 %add_multiply_fusion = f32[2048,2,512]{2,0,1:T(8,128)} fusion(f32[2,2048,512]{2,1,0:T(8,128)} %copy-done.2, bf16[2048,2,128]{0,2,1:T(8,128)(2,1)S(1)} %bitcast.553, pred[]{:T(512)S(6)} %eq.3, bf16[1,2,128,512]{3,2,1,0:T(8,128)(2,1)S(1)} %copy-done.21), kind=kOutput, calls=%fused_computation.10 | convolution fusion | flops 553648128 | bytes 18087936 | tf_op jit(solution)/shard_map/tjq,jqe->tje/dot_general | solution.py:82
  254.7 7.1 %fusion.12 = bf16[2048,2,128]{2,0,1:T(8,128)(2,1)} fusion(f32[2048,2,512]{2,0,1:T(8,128)} %add_multiply_fusion, bf16[2048,4,2,32]{0,3,2,1:T(8,128)(2,1)} %bitcast.551, bf16[1,2,128,512]{3,2,1,0:T(8,128)(2,1)S(1)} %copy-done.21, bf16[2,512,4,32]{1,3,2,0:T(8,128)(2,1)} %bitcast.557), kind=kOutput, calls=%fused_computation.24 | convolution fusion | flops 1078460416 | bytes 11010048 | tf_op jit(solution)/shard_map/tje,jqe->tjq/dot_general | solution.py:139
  261.8 3.7 copy.184
  265.5 4.6 all-to-all-start.8
  271.1 9.8 %all-to-all-done.8 = bf16[2048,2,128]{0,1,2:T(2,128)(2,1)} async-done(((bf16[2048,2,128]{0,1,2:T(2,128)(2,1)}), bf16[2048,2,128]{0,1,2:T(2,128)(2,1)}, u32[]{:S(2)}, u32[]{:S(2)}) %all-to-all-start.8) | async-done | bytes 1048608 | tf_op jit(solution)/shard_map/all_to_all | solution.py:142
  283.1 8.6 %copy.230 = f32[2048,2,128]{2,1,0:T(2,128)} copy(f32[2048,2,128]{2,0,1:T(8,128)S(1)} %convolution_bitcast_fusion.1) | data formatting | bytes 4194304 | tf_op jit(solution)/shard_map/reshape | solution.py:150
  291.6 3.9 reshape.129
  295.5 3.3 multiply_convert_fusion.1
  299.4 20.8 %all_to_all.236 = bf16[8,256,256]{2,0,1:T(8,128)(2,1)S(1)} all-to-all(bf16[8,256,256]{2,0,1:T(8,128)(2,1)S(1)} %copy.191), channel_id=1, replica_groups=mesh['segment'=2,'seq'=32,'mp'=2] {'seq'}, dimensions={1} | all-to-all | bytes 2097152 | tf_op jit(solution)/shard_map/all_to_all | solution.py:38
  323.0 2.6 copy.195
  325.7 17.9 %all_to_all.237 = bf16[256,8,256]{2,1,0:T(8,128)(2,1)S(1)} all-to-all(bf16[256,8,256]{2,1,0:T(8,128)(2,1)} %copy.195), channel_id=1, replica_groups=mesh['segment'=2,'seq'=32,'mp'=2] {'seq'}, dimensions={0} | all-to-all | bytes 2097152 | tf_op jit(solution)/shard_map/all_to_all | solution.py:45
  343.6 6.1 %fusion.14 = bf16[8,256,256]{2,1,0:T(8,128)(2,1)} fusion(f32[8,256,256]{2,0,1:T(8,128)} %bitcast.544, f32[8,256,256]{2,1,0:T(8,128)} %reshape.129, bf16[8,256,256]{2,1,0:T(8,128)(2,1)} %bitcast.517, bf16[1,8,256,256]{3,2,1,0:T(8,128)(2,1)} %param.14, f32[256]{0:T(256)S(1)} %bitcast.566, f32[256]{0:T(256)S(1)} %bitcast.562, ...), kind=kOutput, calls=%fused_computation.28 | convolution fusion | flops 277872640 | bytes 12584961 | tf_op jit(solution)/shard_map/aoi,aoc->aic/dot_general | solution.py:155
  349.7 2.3 copy.198
  351.9 7.2 %collective-permute-start.1 = (bf16[2048,256]{0,1:T(8,128)(2,1)}, bf16[2048,256]{0,1:T(8,128)(2,1)S(1)}, u32[]{:S(2)}, u32[]{:S(2)}) collective-permute-start(bf16[2048,256]{0,1:T(8,128)(2,1)} %copy.198), channel_id=1, source_target_pairs={{64,0},{65,1},{66,2},{67,3},{68,4},{69,5},{70,6},{71,7},{72,8},{73... | collective-permute-start | bytes 3145736 | tf_op jit(solution)/shard_map/ppermute | solution.py:10
  359.2 2.0 collective-permute-done.1
  363.7 3.7 copy.201
  367.4 18.4 %all_to_all.238 = bf16[2048,2,128]{0,1,2:T(2,128)(2,1)S(1)} all-to-all(bf16[2048,2,128]{0,1,2:T(2,128)(2,1)} %copy.201), channel_id=1, replica_groups=mesh['segment'=2,'seq'=32,'mp'=2] {'mp'}, dimensions={2} | all-to-all | bytes 2097152 | tf_op jit(solution)/shard_map/all_to_all | solution.py:132
  387.2 7.1 %fusion.13 = bf16[2048,2,128]{2,0,1:T(8,128)(2,1)} fusion(f32[2048,2,512]{2,0,1:T(8,128)} %add_multiply_fusion, bf16[2048,4,2,32]{0,3,2,1:T(8,128)(2,1)} %bitcast.552, bf16[1,2,128,512]{3,2,1,0:T(8,128)(2,1)S(1)} %copy-done.21, bf16[2,512,4,32]{1,3,2,0:T(8,128)(2,1)} %bitcast.558), kind=kOutput, calls=%fused_computation.25 | convolution fusion | flops 1078460416 | bytes 11010048 | tf_op jit(solution)/shard_map/tje,jqe->tjq/dot_general | solution.py:139
  394.3 3.7 copy.205
  398.0 4.4 all-to-all-start.12
  402.4 2.6 copy.199
  405.0 11.5 %all-to-all-done.12 = bf16[2048,2,128]{0,1,2:T(2,128)(2,1)} async-done(((bf16[2048,2,128]{0,1,2:T(2,128)(2,1)}), bf16[2048,2,128]{0,1,2:T(2,128)(2,1)}, u32[]{:S(2)}, u32[]{:S(2)}) %all-to-all-start.12) | async-done | bytes 1048608 | tf_op jit(solution)/shard_map/all_to_all | solution.py:142
  418.7 8.6 %copy.209 = f32[2048,2,128]{2,1,0:T(2,128)} copy(f32[2048,2,128]{2,0,1:T(8,128)S(1)} %convolution_bitcast_fusion) | data formatting | bytes 4194304 | tf_op jit(solution)/shard_map/tjkc,kijc->tki/transpose | solution.py:145
  427.2 3.9 reshape.107
  431.1 3.5 multiply_convert_fusion
  435.2 18.7 %all_to_all.239 = bf16[8,256,256]{2,0,1:T(8,128)(2,1)S(1)} all-to-all(bf16[8,256,256]{2,0,1:T(8,128)(2,1)S(1)} %copy.210), channel_id=1, replica_groups=mesh['segment'=2,'seq'=32,'mp'=2] {'seq'}, dimensions={1} | all-to-all | bytes 2097152 | tf_op jit(solution)/shard_map/all_to_all | solution.py:38
  456.7 2.8 copy.214
  459.5 4.9 all-to-all-start.14
  464.5 1.9 fusion.49
  468.1 9.9 %all-to-all-done.14 = bf16[256,8,256]{2,1,0:T(8,128)(2,1)} async-done(((bf16[256,8,256]{2,1,0:T(8,128)(2,1)}), bf16[256,8,256]{2,1,0:T(8,128)(2,1)}, u32[]{:S(2)}, u32[]{:S(2)}) %all-to-all-start.14) | async-done | bytes 1048608 | tf_op jit(solution)/shard_map/all_to_all | solution.py:45
  478.0 2.2 fusion.29
  481.8 70.9 %all-reduce.3.cloned.1.call-done = (bf16[1,8,256,256]{3,2,1,0:T(8,128)(2,1)}, bf16[1,8,256,256]{3,2,1,0:T(8,128)(2,1)}) async-done(((bf16[1,8,256,256]{3,2,1,0:T(8,128)(2,1)}, bf16[1,8,256,256]{3,2,1,0:T(8,128)(2,1)}), (bf16[1,8,256,256]{3,2,1,0:T(8,128)(2,1)}, bf16[1,8,256,256]{3,2,1,0:T(8,128)(2,1)})) %all-reduce.3.cloned.1.call-update) | async-done | bytes 2097168 | tf_op jit(solution)/shard_map/psum | solution.py:169
  552.8 2.7 dynamic-slice_convert_fusion
  (159 shorter events, 77.8 us)
Async XLA Ops:
  7.2 31.9 %copy-start = (bf16[1,8,256,256]{3,2,1,0:T(8,128)(2,1)S(1)}, bf16[1,8,256,256]{3,2,1,0:T(8,128)(2,1)}, u32[]{:S(2)}) copy-start(bf16[1,8,256,256]{3,2,1,0:T(8,128)(2,1)} %param.15) | copy-start | bytes 3145732
  7.2 1.5 copy-start.25
  8.7 1.5 copy-start.3
  8.9 1.0 copy-start.5
  39.0 10.4 %copy-start.7 = (bf16[8,256,256]{2,0,1:T(8,128)(2,1)}, bf16[8,256,256]{2,0,1:T(8,128)(2,1)S(1)}, u32[]{:S(2)}) copy-start(bf16[8,256,256]{2,0,1:T(8,128)(2,1)S(1)} %all_to_all.232) | copy-start | bytes 3145732
  59.3 18.9 %all-to-all-start.2 = ((bf16[32,8,8,256]{3,1,2,0:T(8,128)(2,1)}), bf16[32,8,8,256]{3,1,2,0:T(8,128)(2,1)}, u32[]{:S(2)}, u32[]{:S(2)}) async-start(bf16[32,8,8,256]{3,1,2,0:T(8,128)(2,1)} %constant_dynamic-update-slice_fusion), calls=%async_computation.2 | async-start | bytes 2097152 | tf_op jit(solution)/shard_map/all_to_all | solution.py:28
  84.9 4.2 copy-start.24
  89.2 3.0 copy-start.22
  92.9 16.0 %copy-start.21 = (bf16[1,2,128,512]{3,2,1,0:T(8,128)(2,1)S(1)}, bf16[1,2,128,512]{3,2,1,0:T(8,128)(2,1)}, u32[]{:S(2)}) copy-start(bf16[1,2,128,512]{3,2,1,0:T(8,128)(2,1)} %param.17) | copy-start | bytes 786436
  108.9 1.3 copy-start.23
  110.2 3.3 copy-start.2
  113.8 13.2 %copy-start.20 = (bf16[1,2,128,128]{3,2,1,0:T(8,128)(2,1)S(1)}, bf16[1,2,128,128]{3,2,1,0:T(8,128)(2,1)}, u32[]{:S(2)}) copy-start(bf16[1,2,128,128]{3,2,1,0:T(8,128)(2,1)} %param.19) | copy-start | bytes 196612
  127.5 9.1 %collective-permute-start = (bf16[2048,256]{0,1:T(8,128)(2,1)S(1)}, bf16[2048,256]{0,1:T(8,128)(2,1)}, u32[]{:S(2)}, u32[]{:S(2)}) collective-permute-start(bf16[2048,256]{0,1:T(8,128)(2,1)S(1)} %bitcast.548), channel_id=1, source_target_pairs={{0,64},{1,65},{2,66},{3,67},{4,68},{5,69},{6,70},{7,71},{8,72},{9,... | collective-permute-start | bytes 3145736 | tf_op jit(solution)/shard_map/ppermute | solution.py:10
  139.2 2.8 copy-start.4
  141.1 1.0 copy-start.9
  168.4 10.4 %copy-start.11 = (bf16[8,256,256]{2,0,1:T(8,128)(2,1)}, bf16[8,256,256]{2,0,1:T(8,128)(2,1)S(1)}, u32[]{:S(2)}) copy-start(bf16[8,256,256]{2,0,1:T(8,128)(2,1)S(1)} %all_to_all.235) | copy-start | bytes 3145732
  188.7 19.4 %all-to-all-start.6 = ((bf16[32,8,8,256]{3,1,2,0:T(8,128)(2,1)}), bf16[32,8,8,256]{3,1,2,0:T(8,128)(2,1)}, u32[]{:S(2)}, u32[]{:S(2)}) async-start(bf16[32,8,8,256]{3,1,2,0:T(8,128)(2,1)} %constant_dynamic-update-slice_fusion.32), calls=%async_computation.6 | async-start | bytes 2097152 | tf_op jit(solution)/shard_map/all_to_all | solution.py:28
  208.1 21.7 %all-to-all-start = ((bf16[2048,2,128]{0,1,2:T(2,128)(2,1)}), bf16[2048,2,128]{0,1,2:T(2,128)(2,1)}, u32[]{:S(2)}, u32[]{:S(2)}) async-start(bf16[2048,2,128]{0,1,2:T(2,128)(2,1)} %copy.152), calls=%async_computation | async-start | bytes 2097152 | tf_op jit(solution)/shard_map/all_to_all | solution.py:132
  229.8 16.0 %all-to-all-start.7 = ((bf16[2048,4,64]{0,2,1:T(8,128)(2,1)}), bf16[2048,4,64]{0,2,1:T(8,128)(2,1)}, u32[]{:S(2)}, u32[]{:S(2)}) async-start(bf16[2048,4,64]{0,2,1:T(8,128)(2,1)} %bitcast.533), calls=%async_computation.7 | async-start | bytes 2097152 | tf_op jit(solution)/shard_map/all_to_all | solution.py:81
  265.5 15.4 %all-to-all-start.8 = ((bf16[2048,2,128]{0,1,2:T(2,128)(2,1)}), bf16[2048,2,128]{0,1,2:T(2,128)(2,1)}, u32[]{:S(2)}, u32[]{:S(2)}) async-start(bf16[2048,2,128]{0,1,2:T(2,128)(2,1)} %copy.184), calls=%async_computation.8 | async-start | bytes 2097152 | tf_op jit(solution)/shard_map/all_to_all | solution.py:142
  320.5 1.0 copy-start.14
  325.7 17.9 %copy-start.1 = (f32[2048,256]{1,0:T(8,128)S(1)}, f32[2048,256]{1,0:T(8,128)}, u32[]{:S(2)}) copy-start(f32[2048,256]{1,0:T(8,128)} %copy.173) | copy-start | bytes 6291460
  343.6 6.1 %copy-start.18 = (bf16[256,8,256]{2,1,0:T(8,128)(2,1)}, bf16[256,8,256]{2,1,0:T(8,128)(2,1)S(1)}, u32[]{:S(2)}) copy-start(bf16[256,8,256]{2,1,0:T(8,128)(2,1)S(1)} %all_to_all.237) | copy-start | bytes 3145732
  351.9 9.2 %collective-permute-start.1 = (bf16[2048,256]{0,1:T(8,128)(2,1)}, bf16[2048,256]{0,1:T(8,128)(2,1)S(1)}, u32[]{:S(2)}, u32[]{:S(2)}) collective-permute-start(bf16[2048,256]{0,1:T(8,128)(2,1)} %copy.198), channel_id=1, source_target_pairs={{64,0},{65,1},{66,2},{67,3},{68,4},{69,5},{70,6},{71,7},{72,8},{73... | collective-permute-start | bytes 3145736 | tf_op jit(solution)/shard_map/ppermute | solution.py:10
  361.2 1.0 copy-start.16
  398.0 18.5 %all-to-all-start.12 = ((bf16[2048,2,128]{0,1,2:T(2,128)(2,1)}), bf16[2048,2,128]{0,1,2:T(2,128)(2,1)}, u32[]{:S(2)}, u32[]{:S(2)}) async-start(bf16[2048,2,128]{0,1,2:T(2,128)(2,1)} %copy.205), calls=%async_computation.12 | async-start | bytes 2097152 | tf_op jit(solution)/shard_map/all_to_all | solution.py:142
  454.3 1.0 copy-start.17
  456.7 7.7 %copy-start.8 = (bf16[8,256,256]{2,0,1:T(8,128)(2,1)S(1)}, bf16[8,256,256]{2,0,1:T(8,128)(2,1)}, u32[]{:S(2)}) copy-start(bf16[8,256,256]{2,0,1:T(8,128)(2,1)} %copy-done.7) | copy-start | bytes 3145732
  456.7 7.7 %copy-start.12 = (bf16[8,256,256]{2,0,1:T(8,128)(2,1)S(1)}, bf16[8,256,256]{2,0,1:T(8,128)(2,1)}, u32[]{:S(2)}) copy-start(bf16[8,256,256]{2,0,1:T(8,128)(2,1)} %copy-done.11) | copy-start | bytes 3145732
  459.5 18.5 %all-to-all-start.14 = ((bf16[256,8,256]{2,1,0:T(8,128)(2,1)}), bf16[256,8,256]{2,1,0:T(8,128)(2,1)}, u32[]{:S(2)}, u32[]{:S(2)}) async-start(bf16[256,8,256]{2,1,0:T(8,128)(2,1)} %copy.214), calls=%async_computation.14 | async-start | bytes 2097152 | tf_op jit(solution)/shard_map/all_to_all | solution.py:45
  464.4 88.3 %all-reduce.3.cloned.1.call-start = ((), (), s32[]{:S(2)}) async-start(), calls=%async_computation.15 | async-start | bytes 4194304 | tf_op jit(solution)/shard_map/psum | solution.py:169
  464.5 2.0 copy-start.13
  464.5 2.0 copy-start.15
  466.5 11.6 %copy-start.6 = (bf16[8,256,256]{2,1,0:T(8,128)(2,1)S(1)}, bf16[8,256,256]{2,1,0:T(8,128)(2,1)}, u32[]{:S(2)}) copy-start(bf16[8,256,256]{2,1,0:T(8,128)(2,1)} %copy-done.5) | copy-start | bytes 3145732
  478.0 2.2 copy-start.10
  478.0 2.2 copy-start.19
Sparse Core Ops, SparseCore 0:
  482.0 70.7 all-reduce.2
